TPU v7x, 512 devices: a whole 4x4x16 slice. The times are simulated.
512 devices in a mesh: chan: 32 (over z, core), tm: 16 (over y, x).
Axes of the slice: x: 4, y: 4, z: 16, core: 2. Of those that a mesh axis runs over, the one named last changes fastest.
Arguments:
- samples: bfloat16 [2048, 128, 512], P('chan', 'tm'), may hold values from -6 to 6
- valid: int32 [2048, 128], P('chan', 'tm'), may hold values 0 or 1
- offsets: int32 [8], replicated, may hold values from 0 to 31
Outputs:
- correlations: bfloat16 [16, 8, 2048, 512], P('tm', None, 'chan')
All inputs are finite; a program needn't handle non-finite values. No bound on the sum of `valid` on one device may be relied on, other than what follows from the above.
Results may differ from a plain program's by a relative error of at most 0.0045.
Values may be sent and summed in bfloat16 or wider, within the bound.
A program may use at most 64 MiB of HBM per device.

v0:
```python
import math

import jax
import jax.numpy as jnp
from jax import lax
from jax.sharding import PartitionSpec as P

OFFSET_SPAN = 32


def passed_along(value, axis, by):
    length = lax.axis_size(axis)
    pairs = [(i, i + by) for i in range(length) if 0 <= i + by < length]
    return lax.ppermute(value, axis, pairs)


def prefix(value, axis, join, neutral):
    count, mine = (lax.axis_size(axis), lax.axis_index(axis))
    pieces = jax.tree.map(lambda part: lax.all_gather(part, axis), value)
    subtotal = jax.tree.map(
        lambda part, zero: jnp.full_like(part, 0) + jnp.asarray(zero, part.dtype), value, neutral
    )

    def hop(position, subtotal):
        longer = join(subtotal, jax.tree.map(lambda part: part[position], pieces))
        return jax.tree.map(lambda new, old: jnp.where(position < mine, new, old), longer, subtotal)

    return lax.fori_loop(0, count - 1, hop, subtotal)


def forward_table(length):
    bins = length // 2
    rows = jnp.arange(length)
    freqs = jnp.arange(bins) + 1
    angle = jnp.mod(rows[:, None] * freqs[None, :], length).astype(jnp.float32) * (
        2.0 * math.pi / length
    )
    return jnp.concatenate([jnp.cos(angle), -jnp.sin(angle)], axis=1).astype(jnp.bfloat16)


def inverse_table(length):
    bins = length // 2
    freqs = jnp.arange(bins) + 1
    lags = jnp.arange(length)
    angle = jnp.mod(freqs[:, None] * lags[None, :], length).astype(jnp.float32) * (
        2.0 * math.pi / length
    )
    return jnp.concatenate([jnp.cos(angle), -jnp.sin(angle)], axis=0)


def whiten(samples, valid, forward):
    chans, wins, length = samples.shape
    bins = length // 2
    raw = jnp.dot(
        samples.reshape(chans * wins, length), forward, preferred_element_type=jnp.float32
    )
    raw = raw.reshape(chans, wins, 2 * bins)
    real_part = raw[..., :bins]
    imag_part = raw[..., bins:]
    power = real_part * real_part + imag_part * imag_part
    level = jnp.mean(power, axis=-1, keepdims=True)
    scale = valid[..., None].astype(jnp.float32) * lax.rsqrt(power + 0.01 * level + 1e-06)
    return (real_part * scale, imag_part * scale)


def per_device(samples, valid, offsets):
    chans, wins, length = samples.shape
    bins = length // 2
    span = OFFSET_SPAN
    pairs = offsets.shape[0]
    forward = forward_table(length)
    own_re, own_im = whiten(samples, valid, forward)
    edge = passed_along(
        jnp.stack([own_re[:span], own_im[:span]]).astype(jnp.bfloat16), "chan", -1
    ).astype(jnp.float32)
    ext_re = jnp.concatenate([own_re, edge[0]], axis=0)
    ext_im = jnp.concatenate([own_im, edge[1]], axis=0)
    head_re = ext_re[:chans]
    head_im = ext_im[:chans]
    decay = jnp.power(jnp.float32(0.99), (wins - 1 - jnp.arange(wins)).astype(jnp.float32))[
        None, :, None
    ]

    def one_pair(offset):
        part_re = lax.dynamic_slice_in_dim(ext_re, offset, chans, 0)
        part_im = lax.dynamic_slice_in_dim(ext_im, offset, chans, 0)
        cross_re = head_re * part_re + head_im * part_im
        cross_im = head_im * part_re - head_re * part_im
        return (jnp.sum(cross_re * decay, axis=1), jnp.sum(cross_im * decay, axis=1))

    local_re, local_im = lax.map(one_pair, offsets)
    factor = jnp.power(jnp.float32(0.99), jnp.float32(wins))
    inverse = inverse_table(length)

    def combine(earlier, later):
        return (
            earlier[0] * later[2] + later[0],
            earlier[1] * later[2] + later[1],
            earlier[2] * later[2],
        )

    identity = (jnp.zeros_like(local_re), jnp.zeros_like(local_im), jnp.ones((), jnp.float32))
    before_re, before_im, before_factor = prefix(
        (local_re, local_im, factor), "tm", combine, identity
    )
    stack_re = before_re * factor + local_re
    stack_im = before_im * factor + local_im
    joined = jnp.concatenate([stack_re, stack_im], axis=-1).reshape(-1, 2 * bins)
    corr = jnp.dot(
        joined, inverse, precision=lax.Precision.HIGHEST, preferred_element_type=jnp.float32
    )
    corr = corr * bins ** (-0.5)
    return corr.reshape(1, pairs, chans, length).astype(jnp.bfloat16)


def solution(mesh):
    in_specs = (P("chan", "tm", None), P("chan", "tm"), P())
    out_specs = P("tm", None, "chan", None)
    return jax.shard_map(
        per_device, mesh=mesh, in_specs=in_specs, out_specs=out_specs, check_vma=False
    )
```

profile of v0, /device:TPU:1, one launch (start us, length us, event | category | flops | bytes accessed | tf_op | source)
XLA Modules:
  0.0 283.8 jit_solution(10325745634188181848)
XLA Ops:
  6.5 2.2 cosine_convert_fusion
  9.4 0.7 convert_element_type.46
  10.5 8.7 %collective-permute-start = (bf16[2,32,8,256]{3,2,1,0:T(8,128)(2,1)S(1)}, bf16[2,32,8,256]{3,2,1,0:T(8,128)(2,1)S(1)}, u32[]{:S(2)}, u32[]{:S(2)}) collective-permute-start(bf16[2,32,8,256]{3,2,1,0:T(8,128)(2,1)S(1)} %pad_maximum_fusion.3), channel_id=1, source_target_pairs={{16,0},{32,16},{48,32},{64,48},{80,64},{96,80},{112,96},{128,112},... | collective-permute-start | bytes 786440 | tf_op jit(solution)/shard_map/ppermute | solution.py:14
  19.3 1.1 collective-permute-done
  20.6 31.6 %while.30 = (s32[]{:T(128)}, f32[8,64,256]{2,1,0:T(8,128)}, f32[8,64,256]{2,1,0:T(8,128)}, s32[8]{0:T(128)S(1)}, f32[96,8,256]{2,1,0:T(8,128)S(1)}, /*index=5*/f...) while((s32[]{:T(128)}, f32[8,64,256]{2,1,0:T(8,128)}, ...), condition=%wide.region_4.5_spmd.clone.clone, body=%wide.region_1.4_spmd.clone.clone.sunk | while | flops 1277973 | bytes 2491103 | solution.py:91
  20.6 0.7 dynamic_slice.53
  23.9 0.7 bitcast_dynamic-update-slice_fusion.3
  24.6 0.7 dynamic_slice.53
  27.9 0.7 bitcast_dynamic-update-slice_fusion.3
  28.5 0.7 dynamic_slice.53
  31.8 0.7 bitcast_dynamic-update-slice_fusion.3
  32.5 0.7 dynamic_slice.53
  35.8 0.7 bitcast_dynamic-update-slice_fusion.3
  36.4 0.7 dynamic_slice.53
  39.7 0.7 bitcast_dynamic-update-slice_fusion.3
  40.4 0.7 dynamic_slice.53
  43.7 0.7 bitcast_dynamic-update-slice_fusion.3
  44.3 0.7 dynamic_slice.53
  47.6 0.7 bitcast_dynamic-update-slice_fusion.3
  48.3 0.7 dynamic_slice.53
  51.6 0.7 bitcast_dynamic-update-slice_fusion.3
  52.3 0.7 all-gather.5.cloned.1.call-update
  53.0 1.3 dynamic-slice
  54.3 0.7 dynamic-update-slice
  55.0 33.2 %all-reduce = f32[16]{0:T(128)S(1)} all-reduce(f32[16]{0:T(128)S(1)} %dynamic-update-slice), channel_id=1, replica_groups=mesh['chan'=32,'tm'=16] {'tm'}, use_global_device_ids=true, to_apply=%add | all-reduce | flops 16 | bytes 128
  88.2 2.1 fusion.24
  90.4 50.5 %all-gather.7.cloned.1.call-done = f32[128,64,256]{2,1,0:T(8,128)} async-done(((f32[8,64,256]{2,1,0:T(8,128)}), f32[128,64,256]{2,1,0:T(8,128)}) %all-gather.7.cloned.1.call-update) | async-done | bytes 8388624 | tf_op jit(solution)/shard_map/all_gather | solution.py:19
  140.9 88.9 %all-gather.5.cloned.1.call-done = f32[128,64,256]{2,1,0:T(8,128)} async-done(((f32[8,64,256]{2,1,0:T(8,128)}), f32[128,64,256]{2,1,0:T(8,128)}) %all-gather.5.cloned.1.call-update) | async-done | bytes 8388624 | tf_op jit(solution)/shard_map/all_gather | solution.py:19
  229.8 43.1 %while.31 = (s32[]{:T(128)}, f32[8,64,256]{2,1,0:T(8,128)S(1)}, f32[8,64,256]{2,1,0:T(8,128)S(1)}, s32[]{:T(128)}, f32[16]{0:T(128)S(1)}, /*index=5*/f32[16,8,64...) while((s32[]{:T(128)}, f32[8,64,256]{2,1,0:T(8,128)S(1)}, ...), condition=%wide.region_6.7_spmd.clone, body=%wide.region_5.6_spmd.clone.sunk | while | flops 1048580 | bytes 3145861 | solution.py:28
  230.4 2.3 fusion.32
  233.3 2.3 fusion.32
  236.2 2.3 fusion.32
  239.1 2.3 fusion.32
  241.3 0.6 dynamic_slice.55
  241.9 2.3 fusion.32
  244.2 0.6 dynamic_slice.55
  244.8 2.3 fusion.32
  247.7 2.3 fusion.32
  250.5 2.3 fusion.32
  253.4 2.3 fusion.32
  256.3 2.3 fusion.32
  259.2 2.3 fusion.32
  262.0 2.3 fusion.32
  264.9 2.3 fusion.32
  267.8 2.3 fusion.32
  270.7 2.3 fusion.32
  273.0 1.1 multiply_add_fusion
  274.3 2.6 fusion.4
  (57 shorter events, 13.7 us)
Async XLA Ops:
  6.5 2.3 copy-start
  6.5 14.0 %copy-start.2 = (s32[8]{0:T(128)S(1)}, s32[8]{0:T(128)}, u32[]{:S(2)}) copy-start(s32[8]{0:T(128)} %param.9) | copy-start | bytes 100
  6.5 134.4 %all-gather.7.cloned.1.call-start = ((), (), s32[]{:S(2)}) async-start(), calls=%async_computation.1 | async-start | bytes 8912896 | tf_op jit(solution)/shard_map/all_gather | solution.py:19
  10.5 9.9 %collective-permute-start = (bf16[2,32,8,256]{3,2,1,0:T(8,128)(2,1)S(1)}, bf16[2,32,8,256]{3,2,1,0:T(8,128)(2,1)S(1)}, u32[]{:S(2)}, u32[]{:S(2)}) collective-permute-start(bf16[2,32,8,256]{3,2,1,0:T(8,128)(2,1)S(1)} %pad_maximum_fusion.3), channel_id=1, source_target_pairs={{16,0},{32,16},{48,32},{64,48},{80,64},{96,80},{112,96},{128,112},... | collective-permute-start | bytes 786440 | tf_op jit(solution)/shard_map/ppermute | solution.py:14
  52.2 177.6 %all-gather.5.cloned.1.call-start = ((), (), s32[]{:S(2)}) async-start(), calls=%async_computation | async-start | bytes 8912896 | tf_op jit(solution)/shard_map/all_gather | solution.py:19
  88.2 184.7 %copy-start.1 = (f32[8,64,256]{2,1,0:T(8,128)S(1)}, f32[8,64,256]{2,1,0:T(8,128)}, u32[]{:S(2)}) copy-start(f32[8,64,256]{2,1,0:T(8,128)} %get-tuple-element.181) | copy-start | bytes 1572868
Sparse Core Ops, SparseCore 0:
  52.4 88.4 all-gather.6
  143.9 85.8 all-gather.4
where the time goes:
time: 285 us; the launch traced here: 284 us
  waiting for transfers between devices  141 us (49%)
  other arithmetic  45.6 us (16%)
  blocking collectives  33.2 us (12%)
  local copies, waits for them, and re-layouts  21.5 us (8%)
  loops' own time  16.7 us (6%)
  between operations  13.6 us (5%)
  starting transfers between devices  8.79 us (3%)
  matrix products  3.09 us (1%)
    all_gather x2, waiting for transfers between devices, prefix(): pieces = jax.tree.map(lambda part: lax.all_gather(part, axis), value)  139 us
    select_n x15, other arithmetic, hop(): jnp.where(position < mine, new, old)  34 us
    unnamed x1, blocking collectives  33.2 us
    another operation x1, loops' own time, per_device(): local_re, local_im = lax.map(one_pair, offsets)  16.5 us
    dynamic_slice x15, local copies, waits for them, and re-layouts, hop(): longer = join(subtotal, jax.tree.map(lambda part: part[position], pieces))  8.83 us
    ppermute x1, starting transfers between devices, passed_along(): return lax.ppermute(value, axis, pairs)  8.75 us
  transfers between devices with their start and end apart: 3, of which 3 were waited for; matrix products, arithmetic and copies ran while one was open for 1% of the time, Pallas kernels for 0%

commit v1 on v0

v1 whole, which is shorter than its diff:
```python
import functools
import math

import jax
import jax.numpy as jnp
import numpy as np
from jax import lax
from jax.experimental import pallas as pl
from jax.experimental.pallas import tpu as pltpu
from jax.sharding import PartitionSpec as P

OFFSET_SPAN = 32
DECAY = 0.99
MESH = pl.DeviceIdType.MESH
F32 = jnp.float32
BF16 = jnp.bfloat16


def angles(rows, columns, length):
    turn = np.mod(rows[:, None] * columns[None, :], length).astype(np.float32)
    return turn * np.float32(2.0 * math.pi / length)


def forward_table(length):
    angle = angles(np.arange(length), np.arange(length // 2) + 1, length)
    return np.concatenate([np.cos(angle), -np.sin(angle)], axis=1).astype(BF16)


def inverse_table(length):
    angle = angles(np.arange(length // 2) + 1, np.arange(length), length)
    table = np.concatenate([np.cos(angle), -np.sin(angle)], axis=0)
    table = table * np.float32((length // 2) ** -0.5)
    high = table.astype(BF16)
    low = (table - high.astype(np.float32)).astype(BF16)
    return np.stack([high, low])


def kernel(
    n_chan,
    n_tm,
    x_hbm,
    valid_ref,
    offsets_ref,
    forward_hbm,
    inverse_hbm,
    out_ref,
    x,
    x_edge,
    valid_edge,
    forward,
    inverse,
    raw,
    mask,
    white,
    send,
    recv,
    high,
    low,
    done,
    load_sem,
    edge_send,
    edge_recv,
    send_sem,
    recv_sem,
    back_send,
    back_recv,
):
    chan = lax.axis_index("chan")
    me = lax.axis_index("tm")
    span = OFFSET_SPAN
    wins, chans = valid_ref.shape
    rows, length = x.shape
    bins = length // 2
    lanes = 128
    half = bins // lanes
    part = send.shape[2]

    barrier = pltpu.get_barrier_semaphore()

    @pl.loop(1, n_tm)
    def _(step):
        peer = lax.rem(me + step, n_tm)
        pl.semaphore_signal(barrier, inc=1, device_id={"tm": peer}, device_id_type=MESH)

    @pl.when(chan > 0)
    def _():
        pl.semaphore_signal(barrier, inc=1, device_id={"chan": chan - 1}, device_id_type=MESH)

    @pl.when(chan < n_chan - 1)
    def _():
        pl.semaphore_signal(barrier, inc=1, device_id={"chan": chan + 1}, device_id_type=MESH)

    load_x = pltpu.make_async_copy(x_hbm, x, load_sem.at[0])
    load_f = pltpu.make_async_copy(forward_hbm, forward, load_sem.at[1])
    load_i = pltpu.make_async_copy(inverse_hbm, inverse, load_sem.at[2])
    load_x.start()
    load_f.start()
    load_i.start()

    def whiten(source, valid, base, count):
        mask[pl.ds(base, chans), :] = valid[...].astype(F32).T

        def product(i, carry):
            at = pl.multiple_of(i * 128, 128)
            block = jnp.dot(
                source[pl.ds(at, 128), :], forward[...], preferred_element_type=F32
            )
            for l in range(2 * half):
                raw[l, pl.ds(at, 128), :] = block[:, l * lanes : (l + 1) * lanes]
            return carry

        lax.fori_loop(0, count * wins // 128, product, 0)

        def block(i, carry):
            at = pl.multiple_of(i * 8 * wins, 8 * wins)
            to = pl.multiple_of(base + i * 8, 8)
            usable = mask[pl.ds(to, 8), :]
            for w in range(wins):
                values = [raw[l, pl.ds(at + w, 8, stride=wins), :] for l in range(2 * half)]
                power = [
                    values[b] * values[b] + values[half + b] * values[half + b]
                    for b in range(half)
                ]
                level = jnp.sum(sum(power), axis=1, keepdims=True) * (1.0 / bins)
                floor = 0.01 * level + 1e-06
                factor = usable[:, w : w + 1] * (DECAY ** (0.5 * (wins - 1 - w)))
                for b in range(half):
                    scale = factor * lax.rsqrt(power[b] + floor)
                    white[w, b, pl.ds(to, 8), :] = values[b] * scale
                    white[w, half + b, pl.ds(to, 8), :] = values[half + b] * scale
            return carry

        lax.fori_loop(0, count // 8, block, 0)

    load_x.wait()
    load_f.wait()
    whiten(x, valid_ref, 0, chans)

    neighbours = (chan > 0).astype(jnp.int32) + (chan < n_chan - 1).astype(jnp.int32)
    pl.semaphore_wait(barrier, n_tm - 1 + neighbours)

    def edge_copies():
        before = {"chan": lax.max(chan - 1, 0)}
        return (
            pltpu.make_async_remote_copy(
                src_ref=x.at[pl.ds(0, span * wins), :],
                dst_ref=x_edge,
                send_sem=edge_send.at[0],
                recv_sem=edge_recv.at[0],
                device_id=before,
                device_id_type=MESH,
            ),
            pltpu.make_async_remote_copy(
                src_ref=valid_ref,
                dst_ref=valid_edge,
                send_sem=edge_send.at[1],
                recv_sem=edge_recv.at[1],
                device_id=before,
                device_id_type=MESH,
            ),
        )

    @pl.when(chan > 0)
    def _():
        for copy in edge_copies():
            copy.start()

    def piece(phase, owner):
        offset = offsets_ref[owner // 2]
        first = phase * (chans // 2) + lax.rem(owner, 2) * part
        slot = send.at[phase, owner]
        for b in range(half):
            real, imag = [], []
            for c in range(0, part, 8):
                own = pl.multiple_of(first + c, 8)
                other = own + offset
                total_re = jnp.zeros((8, lanes), F32)
                total_im = jnp.zeros((8, lanes), F32)
                for w in range(wins):
                    own_re = white[w, b, pl.ds(own, 8), :]
                    own_im = white[w, half + b, pl.ds(own, 8), :]
                    other_re = white[w, b, pl.ds(other, 8), :]
                    other_im = white[w, half + b, pl.ds(other, 8), :]
                    total_re = total_re + (own_re * other_re + own_im * other_im)
                    total_im = total_im + (own_im * other_re - own_re * other_im)
                real.append(total_re)
                imag.append(total_im)
            slot[:, b * lanes : (b + 1) * lanes] = jnp.concatenate(real, axis=0).astype(BF16)
            slot[:, bins + b * lanes : bins + (b + 1) * lanes] = jnp.concatenate(
                imag, axis=0
            ).astype(BF16)

    def piece_copy(phase, owner):
        return pltpu.make_async_remote_copy(
            src_ref=send.at[phase, owner],
            dst_ref=recv.at[phase, me],
            send_sem=send_sem.at[phase, owner],
            recv_sem=recv_sem.at[phase, me],
            device_id={"tm": owner},
            device_id_type=MESH,
        )

    def piece_arrival(phase, source):
        return pltpu.make_async_remote_copy(
            src_ref=send.at[phase, source],
            dst_ref=recv.at[phase, source],
            send_sem=send_sem.at[phase, source],
            recv_sem=recv_sem.at[phase, source],
            device_id={"tm": source},
            device_id_type=MESH,
        )

    def spread(phase):
        def one(step, carry):
            piece(phase, lax.rem(me + step, n_tm))

            @pl.when(step > 1)
            def _():
                piece_copy(phase, lax.rem(me + step - 1, n_tm)).start()

            return carry

        lax.fori_loop(1, n_tm + 1, one, 0)

    spread(0)

    @pl.when(chan < n_chan - 1)
    def _():
        for copy in edge_copies():
            copy.wait_recv()
        whiten(x_edge, valid_edge, chans, span)

    @pl.when(chan == n_chan - 1)
    def _():
        for w in range(wins):
            for l in range(2 * half):
                white[w, l, chans : chans + span, :] = jnp.zeros((span, lanes), F32)

    spread(1)

    load_i.wait()
    fade = DECAY**wins

    def home(phase):
        return me // 2, phase * (chans // 2) + lax.rem(me, 2) * part

    def back_copy(phase, group):
        pair, first = home(phase)
        return pltpu.make_async_remote_copy(
            src_ref=done.at[phase, group],
            dst_ref=out_ref.at[pair, pl.ds(first, part), :],
            send_sem=back_send.at[phase, group],
            recv_sem=back_recv.at[phase, me],
            device_id={"tm": group},
            device_id_type=MESH,
        )

    def back_arrival(phase, source):
        first = phase * (chans // 2) + lax.rem(source, 2) * part
        return pltpu.make_async_remote_copy(
            src_ref=done.at[phase, source],
            dst_ref=out_ref.at[source // 2, pl.ds(first, part), :],
            send_sem=back_send.at[phase, source],
            recv_sem=back_recv.at[phase, source],
            device_id={"tm": source},
            device_id_type=MESH,
        )

    def finish(phase):
        def scan(group, total):
            @pl.when(group != me)
            def _():
                piece_arrival(phase, group).wait_recv()
                high[pl.ds(group * part, part), :] = recv[phase, group]

            @pl.when(group == me)
            def _():
                high[pl.ds(group * part, part), :] = send[phase, me]

            local = high[pl.ds(group * part, part), :].astype(F32)
            total = total * fade + local
            top = total.astype(BF16)
            high[pl.ds(group * part, part), :] = top
            low[pl.ds(group * part, part), :] = (total - top.astype(F32)).astype(BF16)
            return total

        lax.fori_loop(0, n_tm, scan, jnp.zeros((part, length), F32))

        groups = 128 // part

        def transform(i, carry):
            at = pl.multiple_of(i * 128, 128)
            top = high[pl.ds(at, 128), :]
            lags = jnp.dot(top, inverse[0], preferred_element_type=F32)
            lags += jnp.dot(low[pl.ds(at, 128), :], inverse[0], preferred_element_type=F32)
            lags += jnp.dot(top, inverse[1], preferred_element_type=F32)
            lags = lags.astype(BF16)
            for j in range(groups):
                done[phase, i * groups + j] = lags[j * part : (j + 1) * part]
            return carry

        lax.fori_loop(0, n_tm * part // 128, transform, 0)

        pair, first = home(phase)
        out_ref[pair, pl.ds(pl.multiple_of(first, part), part), :] = done[phase, me]

        @pl.loop(1, n_tm)
        def _(step):
            back_copy(phase, lax.rem(me + step, n_tm)).start()

    finish(0)
    finish(1)

    for phase in range(2):

        @pl.loop(1, n_tm)
        def _(step):
            peer = lax.rem(me + step, n_tm)
            piece_copy(phase, peer).wait_send()
            back_copy(phase, peer).wait_send()

    @pl.when(chan > 0)
    def _():
        for copy in edge_copies():
            copy.wait_send()

    for phase in range(2):

        @pl.loop(1, n_tm)
        def _(step):
            back_arrival(phase, lax.rem(me + n_tm - step, n_tm)).wait_recv()


def per_device(n_chan, n_tm, samples, valid, offsets):
    chans, wins, length = samples.shape
    pairs = offsets.shape[0]
    bins = length // 2
    part = pairs * chans // 2 // n_tm
    rows = chans * wins
    edge = OFFSET_SPAN * wins
    vmem = pltpu.VMEM
    dma = pltpu.SemaphoreType.DMA
    out = pl.pallas_call(
        functools.partial(kernel, n_chan, n_tm),
        out_shape=jax.ShapeDtypeStruct((pairs, chans, length), BF16),
        in_specs=[
            pl.BlockSpec(memory_space=pl.ANY),
            pl.BlockSpec(memory_space=pltpu.VMEM),
            pl.BlockSpec(memory_space=pltpu.SMEM),
            pl.BlockSpec(memory_space=pl.ANY),
            pl.BlockSpec(memory_space=pl.ANY),
        ],
        out_specs=pl.BlockSpec(memory_space=pltpu.VMEM),
        scratch_shapes=[
            vmem((rows, length), BF16),
            vmem((edge, length), BF16),
            vmem((wins, chans), jnp.int32),
            vmem((length, length), BF16),
            vmem((2, length, length), BF16),
            vmem((2 * bins // 128, rows, 128), F32),
            vmem((2 * chans, wins), F32),
            vmem((wins, 2 * bins // 128, chans + OFFSET_SPAN, 128), F32),
            vmem((2, n_tm, part, length), BF16),
            vmem((2, n_tm, part, length), BF16),
            vmem((n_tm * part, length), BF16),
            vmem((n_tm * part, length), BF16),
            vmem((2, n_tm, part, length), BF16),
            dma((3,)),
            dma((2,)),
            dma((2,)),
            dma((2, n_tm)),
            dma((2, n_tm)),
            dma((2, n_tm)),
            dma((2, n_tm)),
        ],
        compiler_params=pltpu.CompilerParams(collective_id=0, has_side_effects=True),
        name="stacks",
    )(
        samples.reshape(rows, length),
        valid.T,
        offsets,
        jnp.asarray(forward_table(length)),
        jnp.asarray(inverse_table(length)),
    )
    return out[None]


def solution(mesh):
    body = functools.partial(per_device, mesh.shape["chan"], mesh.shape["tm"])
    return jax.shard_map(
        body,
        mesh=mesh,
        in_specs=(P("chan", "tm", None), P("chan", "tm"), P()),
        out_specs=P("tm", None, "chan", None),
        check_vma=False,
    )
```

time: 285 us -> 32.4 us (0.11)
  the two profiles are of different devices: /device:TPU:1 before, /device:TPU:101 now
where the time goes in v1:
time: 32.4 us; the launch traced here: 32.2 us
  Pallas kernels  30.3 us (94%)
  local copies, waits for them, and re-layouts  1.87 us (6%)
    pallas_call x1, Pallas kernels, per_device(): pl.pallas_call(functools.partial(kernel, n_chan, n_tm), out_shape=jax.Sha...  30.3 us
    unnamed x1, local copies, waits for them, and re-layouts  1.87 us

profile of v1, /device:TPU:101, one launch (start us, length us, event | category | flops | bytes accessed | tf_op | source)
XLA Modules:
  0.0 32.2 jit_solution(12994650595473132106)
XLA Ops:
  0.0 30.3 %stacks.1 = bf16[8,64,512]{2,1,0:T(8,128)(2,1)} custom-call(bf16[512,512]{1,0:T(8,128)(2,1)} %bitcast.4, s32[8,64]{1,0:T(8,128)} %bitcast.5, s32[8]{0:T(128)} %offsets_ref.1, bf16[512,512]{1,0:T(8,128)(2,1)} %constant.4.clone.forward_hbm, bf16[2,512,512]{2,1,0:T(8,128)(2,1)} %constant.5.clone.inverse_hbm), custom_call_target="tpu_custom_call" | custom-call | tf_op jit(solution)/shard_map/stacks/pallas_call | solution.py:343
  30.3 1.9 %copy.7 = bf16[1,8,64,512]{3,2,1,0:T(8,128)(2,1)} copy(bf16[1,8,64,512]{3,2,1,0:T(8,128)(2,1)} %bitcast.3) | data formatting | bytes 1048576

commit v2 on v1

v2 whole, which is shorter than its diff:
```python
import functools
import math

import jax
import jax.numpy as jnp
import numpy as np
from jax import lax
from jax.experimental import pallas as pl
from jax.experimental.pallas import tpu as pltpu
from jax.sharding import PartitionSpec as P

OFFSET_SPAN = 32
DECAY = 0.99
MESH = pl.DeviceIdType.MESH
F32 = jnp.float32
BF16 = jnp.bfloat16
WHITEN = 16


def angles(rows, columns, length):
    turn = np.mod(rows[:, None] * columns[None, :], length).astype(np.float32)
    return turn * np.float32(2.0 * math.pi / length)


def forward_table(length):
    angle = angles(np.arange(length), np.arange(length // 2) + 1, length)
    return np.concatenate([np.cos(angle), -np.sin(angle)], axis=1).astype(BF16)


def inverse_table(length):
    angle = angles(np.arange(length // 2) + 1, np.arange(length), length)
    table = np.concatenate([np.cos(angle), -np.sin(angle)], axis=0)
    table = table * np.float32((length // 2) ** -0.5)
    high = table.astype(BF16)
    low = (table - high.astype(np.float32)).astype(BF16)
    return np.stack([high, low])


def kernel(
    n_chan,
    n_tm,
    x_hbm,
    valid_ref,
    offsets_ref,
    forward_hbm,
    inverse_hbm,
    out_ref,
    x,
    x_edge,
    valid_edge,
    forward,
    inverse,
    raw,
    mask,
    white,
    send,
    recv,
    lags,
    done,
    load_sem,
    edge_send,
    edge_recv,
    send_sem,
    recv_sem,
    back_send,
    back_recv,
    home_sem,
):
    chan = lax.axis_index("chan")
    me = lax.axis_index("tm")
    span = OFFSET_SPAN
    wins, chans = valid_ref.shape
    pairs = offsets_ref.shape[0]
    rows, length = x.shape
    bins = length // 2
    lanes = 128
    half = bins // lanes
    part = recv.shape[3]
    last = n_tm - 1
    blocks = chans // 16
    share = n_tm // blocks

    barrier = pltpu.get_barrier_semaphore()
    for step in range(1, n_tm):
        peer = (me + step) & last
        pl.semaphore_signal(barrier, inc=1, device_id={"tm": peer}, device_id_type=MESH)

    @pl.when(chan > 0)
    def _():
        pl.semaphore_signal(barrier, inc=1, device_id={"chan": chan - 1}, device_id_type=MESH)

    @pl.when(chan < n_chan - 1)
    def _():
        pl.semaphore_signal(barrier, inc=1, device_id={"chan": chan + 1}, device_id_type=MESH)

    load_x = pltpu.make_async_copy(x_hbm, x, load_sem.at[0])
    load_f = pltpu.make_async_copy(forward_hbm, forward, load_sem.at[1])
    load_i = pltpu.make_async_copy(inverse_hbm, inverse, load_sem.at[2])
    load_x.start()
    load_f.start()
    load_i.start()

    def product(source):
        block = jnp.dot(source[...], forward[...], preferred_element_type=F32)
        for l in range(2 * half):
            raw[l, : source.shape[0], :] = block[:, l * lanes : (l + 1) * lanes]

    def whiten(valid, base, count, group):
        mask[base : base + chans, :] = valid[...].astype(F32).T

        def block(i, carry):
            at = pl.multiple_of(i * group * wins, group * wins)
            to = pl.multiple_of(base + i * group, 8)
            usable = mask[pl.ds(to, group), :]
            for w in range(wins):
                values = [raw[l, pl.ds(at + w, group, stride=wins), :] for l in range(2 * half)]
                power = [
                    values[b] * values[b] + values[half + b] * values[half + b]
                    for b in range(half)
                ]
                level = jnp.sum(sum(power), axis=1, keepdims=True) * (1.0 / bins)
                floor = 0.01 * level + 1e-06
                factor = usable[:, w : w + 1] * (DECAY ** (0.5 * (wins - 1 - w)))
                for b in range(half):
                    scale = factor * lax.rsqrt(power[b] + floor)
                    white[w, b, pl.ds(to, group), :] = values[b] * scale
                    white[w, half + b, pl.ds(to, group), :] = values[half + b] * scale
            return carry

        lax.fori_loop(0, count // group, block, 0)

    def edge_copies():
        before = {"chan": lax.max(chan - 1, 0)}
        return (
            pltpu.make_async_remote_copy(
                src_ref=x.at[pl.ds(0, span * wins), :],
                dst_ref=x_edge,
                send_sem=edge_send.at[0],
                recv_sem=edge_recv.at[0],
                device_id=before,
                device_id_type=MESH,
            ),
            pltpu.make_async_remote_copy(
                src_ref=valid_ref,
                dst_ref=valid_edge,
                send_sem=edge_send.at[1],
                recv_sem=edge_recv.at[1],
                device_id=before,
                device_id_type=MESH,
            ),
        )

    load_x.wait()
    load_f.wait()
    product(x)

    neighbours = (chan > 0).astype(jnp.int32) + (chan < n_chan - 1).astype(jnp.int32)
    pl.semaphore_wait(barrier, n_tm - 1 + neighbours)

    @pl.when(chan > 0)
    def _():
        for copy in edge_copies():
            copy.start()

    whiten(valid_ref, 0, chans, WHITEN)

    def piece(phase, block):
        own = pl.multiple_of(phase * (chans // 2) + block * 8, 8)
        for b in range(half):
            own_re = [white[w, b, pl.ds(own, 8), :] for w in range(wins)]
            own_im = [white[w, half + b, pl.ds(own, 8), :] for w in range(wins)]
            for q in range(share):
                real, imag = [], []
                for k in range(q * (pairs // share), (q + 1) * (pairs // share)):
                    other = own + offsets_ref[k]
                    total_re = jnp.zeros((8, lanes), F32)
                    total_im = jnp.zeros((8, lanes), F32)
                    for w in range(wins):
                        other_re = white[w, b, pl.ds(other, 8), :]
                        other_im = white[w, half + b, pl.ds(other, 8), :]
                        total_re += own_re[w] * other_re + own_im[w] * other_im
                        total_im += own_im[w] * other_re - own_re[w] * other_im
                    real.append(total_re)
                    imag.append(total_im)
                slot = block * share + q
                send[phase, slot, b] = jnp.concatenate(real, axis=0).astype(BF16)
                send[phase, slot, half + b] = jnp.concatenate(imag, axis=0).astype(BF16)

    def piece_copy(phase, owner, source):
        return pltpu.make_async_remote_copy(
            src_ref=send.at[phase, owner],
            dst_ref=recv.at[phase, source],
            send_sem=send_sem.at[phase, owner],
            recv_sem=recv_sem.at[phase, source],
            device_id={"tm": owner},
            device_id_type=MESH,
        )

    def spread(phase):
        def one(step, carry):
            block = ((me >> 2) + step) & (blocks - 1)
            piece(phase, block)
            for q in range(share):
                owner = block * share + ((me + q) & (share - 1))

                @pl.when(owner != me)
                def _():
                    piece_copy(phase, owner, me).start()

            return carry

        lax.fori_loop(1, blocks + 1, one, 0)

    spread(0)

    @pl.when(chan < n_chan - 1)
    def _():
        for copy in edge_copies():
            copy.wait_recv()
        product(x_edge)
        whiten(valid_edge, chans, span, WHITEN)

    @pl.when(chan == n_chan - 1)
    def _():
        for w in range(wins):
            for l in range(2 * half):
                white[w, l, chans : chans + span, :] = jnp.zeros((span, lanes), F32)

    spread(1)

    load_i.wait()
    fade = DECAY**wins
    per = pairs // share

    def home(phase, owner):
        first = phase * (chans // 2) + (owner >> 2) * 8
        return out_ref.at[pl.ds((owner & (share - 1)) * per, per), pl.ds(first, 8), :]

    def back_copy(phase, group, owner):
        return pltpu.make_async_remote_copy(
            src_ref=done.at[phase, group],
            dst_ref=home(phase, owner),
            send_sem=back_send.at[phase, group],
            recv_sem=back_recv.at[phase, owner],
            device_id={"tm": group},
            device_id_type=MESH,
        )

    def home_copy(phase):
        return pltpu.make_async_copy(done.at[phase, me], home(phase, me), home_sem.at[phase])

    def finish(phase):
        recv[phase, me] = send[phase, me]

        @pl.loop(1, n_tm)
        def _(step):
            source = (me - step) & last
            piece_copy(phase, source, source).wait_recv()

        total = None
        for b in range(0, 2 * half, 2):
            block = jnp.concatenate(
                [recv[phase, :, b + i].reshape(n_tm * part, lanes) for i in range(2)], axis=1
            )
            for t in range(2):
                term = jnp.dot(
                    block,
                    inverse[t, b * lanes : (b + 2) * lanes, :],
                    preferred_element_type=F32,
                )
                total = term if total is None else total + term
        lags[...] = total
        state = jnp.zeros((part, length), F32)
        for group in range(n_tm):
            state = state * fade + lags[group * part : (group + 1) * part, :]
            done[phase, group] = state.astype(BF16).reshape(per, 8, length)

        for step in range(1, n_tm):
            back_copy(phase, (me + step) & last, me).start()
        home_copy(phase).start()

    finish(0)
    finish(1)

    for phase in range(2):

        @pl.loop(1, n_tm)
        def _(step):
            peer = (me + step) & last
            piece_copy(phase, peer, me).wait_send()
            back_copy(phase, peer, me).wait_send()

        home_copy(phase).wait()

    @pl.when(chan > 0)
    def _():
        for copy in edge_copies():
            copy.wait_send()

    for phase in range(2):

        @pl.loop(1, n_tm)
        def _(step):
            source = (me - step) & last
            back_copy(phase, source, source).wait_recv()


def per_device(n_chan, n_tm, samples, valid, offsets):
    chans, wins, length = samples.shape
    pairs = offsets.shape[0]
    bins = length // 2
    part = pairs * chans // 2 // n_tm
    rows = chans * wins
    edge = OFFSET_SPAN * wins
    vmem = pltpu.VMEM
    dma = pltpu.SemaphoreType.DMA
    out = pl.pallas_call(
        functools.partial(kernel, n_chan, n_tm),
        out_shape=jax.ShapeDtypeStruct((pairs, chans, length), BF16),
        in_specs=[
            pl.BlockSpec(memory_space=pl.ANY),
            pl.BlockSpec(memory_space=pltpu.VMEM),
            pl.BlockSpec(memory_space=pltpu.SMEM),
            pl.BlockSpec(memory_space=pl.ANY),
            pl.BlockSpec(memory_space=pl.ANY),
        ],
        out_specs=pl.BlockSpec(memory_space=pl.ANY),
        scratch_shapes=[
            vmem((rows, length), BF16),
            vmem((edge, length), BF16),
            vmem((wins, chans), jnp.int32),
            vmem((length, length), BF16),
            vmem((2, length, length), BF16),
            vmem((2 * bins // 128, rows, 128), F32),
            vmem((2 * chans, wins), F32),
            vmem((wins, 2 * bins // 128, chans + OFFSET_SPAN, 128), F32),
            vmem((2, n_tm, length // 128, part, 128), BF16),
            vmem((2, n_tm, length // 128, part, 128), BF16),
            vmem((n_tm * part, length), F32),
            vmem((2, n_tm, part // 8, 8, length), BF16),
            dma((3,)),
            dma((2,)),
            dma((2,)),
            dma((2, n_tm)),
            dma((2, n_tm)),
            dma((2, n_tm)),
            dma((2, n_tm)),
            dma((2,)),
        ],
        compiler_params=pltpu.CompilerParams(collective_id=0, has_side_effects=True),
        name="stacks",
    )(
        samples.reshape(rows, length),
        valid.T,
        offsets,
        jnp.asarray(forward_table(length)),
        jnp.asarray(inverse_table(length)),
    )
    return out[None]


def solution(mesh):
    body = functools.partial(per_device, mesh.shape["chan"], mesh.shape["tm"])
    return jax.shard_map(
        body,
        mesh=mesh,
        in_specs=(P("chan", "tm", None), P("chan", "tm"), P()),
        out_specs=P("tm", None, "chan", None),
        check_vma=False,
    )
```

time: 32.4 us -> 30.5 us (0.941)
  the two profiles are of different devices: /device:TPU:101 before, /device:TPU:229 now
where the time goes in v2:
time: 30.5 us; the launch traced here: 30.3 us
  Pallas kernels  28.4 us (93%)
  local copies, waits for them, and re-layouts  1.87 us (6%)
    pallas_call x1, Pallas kernels, per_device(): pl.pallas_call(functools.partial(kernel, n_chan, n_tm), out_shape=jax.Sha...  28.4 us
    unnamed x1, local copies, waits for them, and re-layouts  1.87 us

profile of v2, /device:TPU:229, one launch (start us, length us, event | category | flops | bytes accessed | tf_op | source)
XLA Modules:
  0.0 30.3 jit_solution(6280089918515569281)
XLA Ops:
  0.0 28.4 %stacks.1 = bf16[8,64,512]{2,1,0:T(8,128)(2,1)} custom-call(bf16[512,512]{1,0:T(8,128)(2,1)} %bitcast.4, s32[8,64]{1,0:T(8,128)} %bitcast.5, s32[8]{0:T(128)} %offsets_ref.1, bf16[512,512]{1,0:T(8,128)(2,1)} %constant.4.clone.forward_hbm, bf16[2,512,512]{2,1,0:T(8,128)(2,1)} %constant.5.clone.inverse_hbm), custom_call_target="tpu_custom_call" | custom-call | tf_op jit(solution)/shard_map/stacks/pallas_call | solution.py:317
  28.4 1.9 %copy.7 = bf16[1,8,64,512]{3,2,1,0:T(8,128)(2,1)} copy(bf16[1,8,64,512]{3,2,1,0:T(8,128)(2,1)} %bitcast.3) | data formatting | bytes 1048576

commit v3 on v2

--- a/solution.py
+++ b/solution.py
@@ -15,6 +15,7 @@
 F32 = jnp.float32
 BF16 = jnp.bfloat16
 WHITEN = 16
+FAR_FIRST = (10, 2, 8, 6, 14, 9, 11, 5, 7, 13, 15, 1, 3, 4, 12)
 
 
 def angles(rows, columns, length):
@@ -40,11 +41,13 @@
     n_chan,
     n_tm,
     x_hbm,
-    valid_ref,
-    offsets_ref,
+    valid_hbm,
+    offsets_hbm,
     forward_hbm,
     inverse_hbm,
     out_ref,
+    valid_ref,
+    offsets_ref,
     x,
     x_edge,
     valid_edge,
@@ -80,9 +83,24 @@
     blocks = chans // 16
     share = n_tm // blocks
 
+    loads = [
+        pltpu.make_async_copy(source, target, load_sem.at[i])
+        for i, (source, target) in enumerate(
+            (
+                (x_hbm, x),
+                (forward_hbm, forward),
+                (valid_hbm, valid_ref),
+                (offsets_hbm, offsets_ref),
+                (inverse_hbm, inverse),
+            )
+        )
+    ]
+    for load in loads:
+        load.start()
+
     barrier = pltpu.get_barrier_semaphore()
-    for step in range(1, n_tm):
-        peer = (me + step) & last
+    for step in FAR_FIRST:
+        peer = (me ^ step) & last
         pl.semaphore_signal(barrier, inc=1, device_id={"tm": peer}, device_id_type=MESH)
 
     @pl.when(chan > 0)
@@ -92,25 +110,16 @@
     @pl.when(chan < n_chan - 1)
     def _():
         pl.semaphore_signal(barrier, inc=1, device_id={"chan": chan + 1}, device_id_type=MESH)
-
-    load_x = pltpu.make_async_copy(x_hbm, x, load_sem.at[0])
-    load_f = pltpu.make_async_copy(forward_hbm, forward, load_sem.at[1])
-    load_i = pltpu.make_async_copy(inverse_hbm, inverse, load_sem.at[2])
-    load_x.start()
-    load_f.start()
-    load_i.start()
 
     def product(source):
         block = jnp.dot(source[...], forward[...], preferred_element_type=F32)
         for l in range(2 * half):
-            raw[l, : source.shape[0], :] = block[:, l * lanes : (l + 1) * lanes]
-
-    def whiten(valid, base, count, group):
-        mask[base : base + chans, :] = valid[...].astype(F32).T
-
+            raw[l, : block.shape[0], :] = block[:, l * lanes : (l + 1) * lanes]
+
+    def whiten(base, count, group):
         def block(i, carry):
             at = pl.multiple_of(i * group * wins, group * wins)
-            to = pl.multiple_of(base + i * group, 8)
+            to = pl.multiple_of(base + i * group, group)
             usable = mask[pl.ds(to, group), :]
             for w in range(wins):
                 values = [raw[l, pl.ds(at + w, group, stride=wins), :] for l in range(2 * half)]
@@ -129,40 +138,50 @@
 
         lax.fori_loop(0, count // group, block, 0)
 
-    def edge_copies():
-        before = {"chan": lax.max(chan - 1, 0)}
-        return (
-            pltpu.make_async_remote_copy(
-                src_ref=x.at[pl.ds(0, span * wins), :],
-                dst_ref=x_edge,
-                send_sem=edge_send.at[0],
-                recv_sem=edge_recv.at[0],
-                device_id=before,
-                device_id_type=MESH,
-            ),
-            pltpu.make_async_remote_copy(
-                src_ref=valid_ref,
-                dst_ref=valid_edge,
-                send_sem=edge_send.at[1],
-                recv_sem=edge_recv.at[1],
-                device_id=before,
-                device_id_type=MESH,
-            ),
+    before = {"chan": lax.max(chan - 1, 0)}
+    flags = pltpu.make_async_remote_copy(
+        src_ref=valid_ref,
+        dst_ref=valid_edge,
+        send_sem=edge_send.at[span // 8],
+        recv_sem=edge_recv.at[span // 8],
+        device_id=before,
+        device_id_type=MESH,
+    )
+
+    def edge_copy(i):
+        at = pl.ds(pl.multiple_of(i * 8 * wins, 8 * wins), 8 * wins)
+        return pltpu.make_async_remote_copy(
+            src_ref=x.at[at, :],
+            dst_ref=x_edge.at[at, :],
+            send_sem=edge_send.at[i],
+            recv_sem=edge_recv.at[i],
+            device_id=before,
+            device_id_type=MESH,
         )
 
-    load_x.wait()
-    load_f.wait()
+    loads[0].wait()
+    loads[1].wait()
     product(x)
+    loads[2].wait()
+    loads[3].wait()
 
     neighbours = (chan > 0).astype(jnp.int32) + (chan < n_chan - 1).astype(jnp.int32)
     pl.semaphore_wait(barrier, n_tm - 1 + neighbours)
 
     @pl.when(chan > 0)
     def _():
-        for copy in edge_copies():
-            copy.start()
-
-    whiten(valid_ref, 0, chans, WHITEN)
+        flags.start()
+        for i in range(span // 8):
+            edge_copy(i).start()
+
+    mask[:chans, :] = valid_ref[...].astype(F32).T
+    whiten(0, chans, WHITEN)
+
+    def owner_of(block, q):
+        return q * share + ((block - q) & (share - 1))
+
+    def block_of(owner):
+        return ((owner >> 2) + owner) & (share - 1)
 
     def piece(phase, block):
         own = pl.multiple_of(phase * (chans // 2) + block * 8, 8)
@@ -182,7 +201,7 @@
                         total_im += own_im[w] * other_re - own_re[w] * other_im
                     real.append(total_re)
                     imag.append(total_im)
-                slot = block * share + q
+                slot = owner_of(block, q)
                 send[phase, slot, b] = jnp.concatenate(real, axis=0).astype(BF16)
                 send[phase, slot, half + b] = jnp.concatenate(imag, axis=0).astype(BF16)
 
@@ -196,29 +215,25 @@
             device_id_type=MESH,
         )
 
-    def spread(phase):
-        def one(step, carry):
-            block = ((me >> 2) + step) & (blocks - 1)
-            piece(phase, block)
-            for q in range(share):
-                owner = block * share + ((me + q) & (share - 1))
-
-                @pl.when(owner != me)
-                def _():
-                    piece_copy(phase, owner, me).start()
-
-            return carry
-
-        lax.fori_loop(1, blocks + 1, one, 0)
-
-    spread(0)
+    def deliver(phase, block):
+        piece(phase, block)
+        for i in range(share):
+            owner = owner_of(block, (me + i) & (share - 1))
+
+            @pl.when(owner != me)
+            def _():
+                piece_copy(phase, owner, me).start()
+
+    def inner(step, carry):
+        deliver(0, (block_of(me) + step) & (blocks - 1))
+        return carry
+
+    lax.fori_loop(1, blocks + 1, inner, 0)
 
     @pl.when(chan < n_chan - 1)
     def _():
-        for copy in edge_copies():
-            copy.wait_recv()
-        product(x_edge)
-        whiten(valid_edge, chans, span, WHITEN)
+        flags.wait_recv()
+        mask[chans:, :] = valid_edge[...].astype(F32).T
 
     @pl.when(chan == n_chan - 1)
     def _():
@@ -226,15 +241,25 @@
             for l in range(2 * half):
                 white[w, l, chans : chans + span, :] = jnp.zeros((span, lanes), F32)
 
-    spread(1)
-
-    load_i.wait()
+    def outer(block, carry):
+        @pl.when(chan < n_chan - 1)
+        def _():
+            edge_copy(block).wait_recv()
+            product(x_edge.at[pl.ds(pl.multiple_of(block * 8 * wins, 8 * wins), 8 * wins), :])
+            whiten(chans + block * 8, 8, 8)
+
+        deliver(1, block)
+        return carry
+
+    lax.fori_loop(0, blocks, outer, 0)
+
+    loads[4].wait()
     fade = DECAY**wins
     per = pairs // share
 
     def home(phase, owner):
-        first = phase * (chans // 2) + (owner >> 2) * 8
-        return out_ref.at[pl.ds((owner & (share - 1)) * per, per), pl.ds(first, 8), :]
+        first = phase * (chans // 2) + block_of(owner) * 8
+        return out_ref.at[pl.ds((owner >> 2) * per, per), pl.ds(first, 8), :]
 
     def back_copy(phase, group, owner):
         return pltpu.make_async_remote_copy(
@@ -294,8 +319,9 @@
 
     @pl.when(chan > 0)
     def _():
-        for copy in edge_copies():
-            copy.wait_send()
+        flags.wait_send()
+        for i in range(span // 8):
+            edge_copy(i).wait_send()
 
     for phase in range(2):
 
@@ -316,16 +342,12 @@
     dma = pltpu.SemaphoreType.DMA
     out = pl.pallas_call(
         functools.partial(kernel, n_chan, n_tm),
-        out_shape=jax.ShapeDtypeStruct((pairs, chans, length), BF16),
-        in_specs=[
-            pl.BlockSpec(memory_space=pl.ANY),
-            pl.BlockSpec(memory_space=pltpu.VMEM),
-            pl.BlockSpec(memory_space=pltpu.SMEM),
-            pl.BlockSpec(memory_space=pl.ANY),
-            pl.BlockSpec(memory_space=pl.ANY),
-        ],
+        out_shape=pltpu.VMEM((pairs, chans, length), BF16),
+        in_specs=[pl.BlockSpec(memory_space=pltpu.HBM)] * 5,
         out_specs=pl.BlockSpec(memory_space=pl.ANY),
         scratch_shapes=[
+            vmem((wins, chans), jnp.int32),
+            pltpu.SMEM((pairs,), jnp.int32),
             vmem((rows, length), BF16),
             vmem((edge, length), BF16),
             vmem((wins, chans), jnp.int32),
@@ -338,16 +360,18 @@
             vmem((2, n_tm, length // 128, part, 128), BF16),
             vmem((n_tm * part, length), F32),
             vmem((2, n_tm, part // 8, 8, length), BF16),
-            dma((3,)),
-            dma((2,)),
-            dma((2,)),
+            dma((5,)),
+            dma((OFFSET_SPAN // 8 + 1,)),
+            dma((OFFSET_SPAN // 8 + 1,)),
             dma((2, n_tm)),
             dma((2, n_tm)),
             dma((2, n_tm)),
             dma((2, n_tm)),
             dma((2,)),
         ],
-        compiler_params=pltpu.CompilerParams(collective_id=0, has_side_effects=True),
+        compiler_params=pltpu.CompilerParams(
+            collective_id=0, has_side_effects=True
+        ),
         name="stacks",
     )(
         samples.reshape(rows, length),

time: 30.5 us -> 28.6 us (0.938)
  the two profiles are of different devices: /device:TPU:229 before, /device:TPU:101 now
where the time goes in v3:
time: 28.6 us; the launch traced here: 28.5 us
  Pallas kernels  27.7 us (97%)
  local copies, waits for them, and re-layouts  0.8 us (3%)
    pallas_call x1, Pallas kernels, per_device(): pl.pallas_call(functools.partial(kernel, n_chan, n_tm), out_shape=pltpu.V...  27.7 us
    unnamed x1, local copies, waits for them, and re-layouts  0.8 us

profile of v3, /device:TPU:101, one launch (start us, length us, event | category | flops | bytes accessed | tf_op | source)
XLA Modules:
  0.0 28.5 jit_solution(4111854364282103985)
XLA Ops:
  0.0 27.7 %stacks.1 = bf16[8,64,512]{2,1,0:T(8,128)(2,1)S(1)} custom-call(bf16[512,512]{1,0:T(8,128)(2,1)} %bitcast.4, s32[8,64]{1,0:T(8,128)} %bitcast.5, s32[8]{0:T(128)} %offsets_hbm.1, bf16[512,512]{1,0:T(8,128)(2,1)} %constant.4.clone.forward_hbm, bf16[2,512,512]{2,1,0:T(8,128)(2,1)} %constant.5.clone.inverse_hbm), custom_call_target="tpu_custom_call" | custom-call | tf_op jit(solution)/shard_map/stacks/pallas_call | solution.py:343
  27.7 0.8 %copy.7 = bf16[1,8,64,512]{3,2,1,0:T(8,128)(2,1)} copy(bf16[1,8,64,512]{3,2,1,0:T(8,128)(2,1)S(1)} %bitcast.3) | data formatting | bytes 1048576

commit v4 on v3

--- a/solution.py
+++ b/solution.py
@@ -164,6 +164,8 @@
     product(x)
     loads[2].wait()
     loads[3].wait()
+    mask[:chans, :] = valid_ref[...].astype(F32).T
+    whiten(0, chans, WHITEN)
 
     neighbours = (chan > 0).astype(jnp.int32) + (chan < n_chan - 1).astype(jnp.int32)
     pl.semaphore_wait(barrier, n_tm - 1 + neighbours)
@@ -174,14 +176,12 @@
         for i in range(span // 8):
             edge_copy(i).start()
 
-    mask[:chans, :] = valid_ref[...].astype(F32).T
-    whiten(0, chans, WHITEN)
 
     def owner_of(block, q):
-        return q * share + ((block - q) & (share - 1))
+        return q * share + block
 
     def block_of(owner):
-        return ((owner >> 2) + owner) & (share - 1)
+        return owner & 3
 
     def piece(phase, block):
         own = pl.multiple_of(phase * (chans // 2) + block * 8, 8)

time: 28.6 us -> 28.2 us (0.986)
  the two profiles are of different devices: /device:TPU:101 before, /device:TPU:225 now
where the time goes in v4:
time: 28.2 us; the launch traced here: 28.1 us
  Pallas kernels  27.3 us (97%)
  local copies, waits for them, and re-layouts  0.8 us (3%)
    pallas_call x1, Pallas kernels, per_device(): pl.pallas_call(functools.partial(kernel, n_chan, n_tm), out_shape=pltpu.V...  27.3 us
    unnamed x1, local copies, waits for them, and re-layouts  0.8 us

profile of v4, /device:TPU:225, one launch (start us, length us, event | category | flops | bytes accessed | tf_op | source)
XLA Modules:
  0.0 28.1 jit_solution(17135223168222585570)
XLA Ops:
  0.0 27.3 %stacks.1 = bf16[8,64,512]{2,1,0:T(8,128)(2,1)S(1)} custom-call(bf16[512,512]{1,0:T(8,128)(2,1)} %bitcast.4, s32[8,64]{1,0:T(8,128)} %bitcast.5, s32[8]{0:T(128)} %offsets_hbm.1, bf16[512,512]{1,0:T(8,128)(2,1)} %constant.4.clone.forward_hbm, bf16[2,512,512]{2,1,0:T(8,128)(2,1)} %constant.5.clone.inverse_hbm), custom_call_target="tpu_custom_call" | custom-call | tf_op jit(solution)/shard_map/stacks/pallas_call | solution.py:343
  27.3 0.8 %copy.7 = bf16[1,8,64,512]{3,2,1,0:T(8,128)(2,1)} copy(bf16[1,8,64,512]{3,2,1,0:T(8,128)(2,1)S(1)} %bitcast.3) | data formatting | bytes 1048576

commit v5 on v4

--- a/solution.py
+++ b/solution.py
@@ -300,12 +300,27 @@
             state = state * fade + lags[group * part : (group + 1) * part, :]
             done[phase, group] = state.astype(BF16).reshape(per, 8, length)
 
+
+    def give(phase):
         for step in range(1, n_tm):
             back_copy(phase, (me + step) & last, me).start()
         home_copy(phase).start()
 
+    early = (chan & 1) == 1
     finish(0)
+
+    @pl.when(early)
+    def _():
+        give(0)
+
     finish(1)
+
+    @pl.when(jnp.logical_not(early))
+    def _():
+        give(0)
+
+    give(1)
+
 
     for phase in range(2):
 

time: 28.2 us -> 27.7 us (0.982)
  Pallas kernels: 27.3 us -> 26.8 us
    pallas_call x1, Pallas kernels: 27.3 us -> 26.8 us  [per_device(): pl.pallas_call(functools.partial(kernel, n_chan, n_tm), out_shape=pltpu.V...]
where the time goes in v5:
time: 27.7 us; the launch traced here: 27.6 us
  Pallas kernels  26.8 us (97%)
  local copies, waits for them, and re-layouts  0.8 us (3%)
    pallas_call x1, Pallas kernels, per_device(): pl.pallas_call(functools.partial(kernel, n_chan, n_tm), out_shape=pltpu.V...  26.8 us
    unnamed x1, local copies, waits for them, and re-layouts  0.8 us

profile of v5, /device:TPU:225, one launch (start us, length us, event | category | flops | bytes accessed | tf_op | source)
XLA Modules:
  0.0 27.6 jit_solution(5039709282718205701)
XLA Ops:
  0.0 26.8 %stacks.1 = bf16[8,64,512]{2,1,0:T(8,128)(2,1)S(1)} custom-call(bf16[512,512]{1,0:T(8,128)(2,1)} %bitcast.4, s32[8,64]{1,0:T(8,128)} %bitcast.5, s32[8]{0:T(128)} %offsets_hbm.1, bf16[512,512]{1,0:T(8,128)(2,1)} %constant.4.clone.forward_hbm, bf16[2,512,512]{2,1,0:T(8,128)(2,1)} %constant.5.clone.inverse_hbm), custom_call_target="tpu_custom_call" | custom-call | tf_op jit(solution)/shard_map/stacks/pallas_call | solution.py:358
  26.8 0.8 %copy.7 = bf16[1,8,64,512]{3,2,1,0:T(8,128)(2,1)} copy(bf16[1,8,64,512]{3,2,1,0:T(8,128)(2,1)S(1)} %bitcast.3) | data formatting | bytes 1048576

commit v6 on v5

--- a/solution.py
+++ b/solution.py
@@ -306,7 +306,7 @@
             back_copy(phase, (me + step) & last, me).start()
         home_copy(phase).start()
 
-    early = (chan & 1) == 1
+    early = jnp.logical_or((chan & 1) == 1, chan == 0)
     finish(0)
 
     @pl.when(early)

time: 27.7 us -> 27.7 us (level)
  no operation moved by 1% of the time
where the time goes in v6:
time: 27.7 us; the launch traced here: 27.6 us
  Pallas kernels  26.8 us (97%)
  local copies, waits for them, and re-layouts  0.8 us (3%)
    pallas_call x1, Pallas kernels, per_device(): pl.pallas_call(functools.partial(kernel, n_chan, n_tm), out_shape=pltpu.V...  26.8 us
    unnamed x1, local copies, waits for them, and re-layouts  0.8 us

profile of v6, /device:TPU:225, one launch (start us, length us, event | category | flops | bytes accessed | tf_op | source)
XLA Modules:
  0.0 27.6 jit_solution(14603485137768376645)
XLA Ops:
  0.0 26.8 %stacks.1 = bf16[8,64,512]{2,1,0:T(8,128)(2,1)S(1)} custom-call(bf16[512,512]{1,0:T(8,128)(2,1)} %bitcast.4, s32[8,64]{1,0:T(8,128)} %bitcast.5, s32[8]{0:T(128)} %offsets_hbm.1, bf16[512,512]{1,0:T(8,128)(2,1)} %constant.4.clone.forward_hbm, bf16[2,512,512]{2,1,0:T(8,128)(2,1)} %constant.5.clone.inverse_hbm), custom_call_target="tpu_custom_call" | custom-call | tf_op jit(solution)/shard_map/stacks/pallas_call | solution.py:358
  26.8 0.8 %copy.7 = bf16[1,8,64,512]{3,2,1,0:T(8,128)(2,1)} copy(bf16[1,8,64,512]{3,2,1,0:T(8,128)(2,1)S(1)} %bitcast.3) | data formatting | bytes 1048576
